TPU v7x, 32 devices: a whole 2x2x4 slice. The times are simulated.
32 devices in a mesh: sec: 2 (over x), tile: 16 (over z, y, core).
Axes of the slice: x: 2, y: 2, z: 4, core: 2. Of those that a mesh axis runs over, the one named last changes fastest.
Arguments:
- start_modes: bfloat16 [16, 24, 384, 384], P('sec', None, 'tile'), may hold values from -6 to 6
- permittivity: bfloat16 [16, 384, 384], P('sec', 'tile'), may hold values from 1 to 12
- heights: int32 [16], replicated, may hold values from 192 to 384, as said below
Outputs:
- mode_fields: bfloat16 [16, 24, 384, 384], P('sec', None, 'tile')
- coupling: float32 [16, 24, 24], P('sec')
Inputs may be any that keep to these rules, and one draw needn't show every extreme that they name: heights[s] is the number of rows in use of section s, counted from row 0; some section uses all 384 rows.
All inputs are finite; a program needn't handle non-finite values.
Results may differ from a plain program's by a relative error of at most 0.001.
Values may be sent and summed in bfloat16 or wider, within the bound.
A program may use at most 128 MiB of HBM per device.

v0:
```python
import math

import jax
import jax.numpy as jnp
from jax import lax
from jax.sharding import PartitionSpec as P

STEPS = 3
DEG = 4


SHIFT_DIAG = 3.0
EPS_WEIGHT = 0.25
LOWER_EDGE = 2.0
UPPER_EDGE = 10.75


def extended(x, sides, width):
    for axis, dim in sides:
        size, length = (lax.axis_size(axis), x.shape[dim])
        up = [(i, (i + 1) % size) for i in range(size - 1)]
        down = [(j, i) for i, j in up]
        last = lax.slice_in_dim(x, length - width, length, axis=dim)
        initial = lax.slice_in_dim(x, 0, width, axis=dim)
        before = lax.ppermute(last, axis, up)
        after = lax.ppermute(initial, axis, down)
        x = jnp.concatenate([before, x, after], axis=dim)
    return x


def passed_along(value, axis, steps):
    count = lax.axis_size(axis)
    initial, last = (max(0, -steps), min(count, count - steps))
    return lax.ppermute(value, axis, [(source, source + steps) for source in range(initial, last)])


def chebyshev_terms(degree):
    center = 0.5 * (UPPER_EDGE + LOWER_EDGE)
    radius = 0.5 * (UPPER_EDGE - LOWER_EDGE)
    anchor = -center / radius
    values = [1.0, anchor]
    for order in range(1, degree):
        values.append(2.0 * anchor * values[order] - values[order - 1])
    return (center, radius, values)


def scaled_apply(padded, field, diag_scaled, row_mask, inverse):
    sided = jnp.pad(field, ((0, 0), (0, 0), (0, 0), (1, 1)))
    beside = padded[:, :, 2:, :] + padded[:, :, :-2, :] + sided[:, :, :, 2:] + sided[:, :, :, :-2]
    return (diag_scaled * field - inverse * beside) * row_mask


def filter_steps(field, apply_once, degree):
    center, radius, values = chebyshev_terms(degree)
    previous = field
    current = apply_once(field) * (1.0 / values[1])
    for order in range(1, degree):
        upcoming = apply_once(current) * (2.0 * values[order] / values[order + 1]) - previous * (
            values[order - 1] / values[order + 1]
        )
        previous = current
        current = upcoming
    return current


def orthonormal(field):
    local = jnp.einsum("smrc,snrc->smn", field, field, precision=lax.Precision.HIGHEST)
    gram = lax.psum(local, "tile")
    lower = jnp.linalg.cholesky(gram)
    flat = field.reshape(field.shape[0], field.shape[1], -1)
    solved = lax.linalg.triangular_solve(lower, flat, left_side=True, lower=True)
    return solved.reshape(field.shape)


def per_device(start_modes, permittivity, heights):
    sec_dev = start_modes.shape[0]
    strip = start_modes.shape[2]
    columns = start_modes.shape[3]
    total_sections = heights.shape[0]
    sec_base = lax.axis_index("sec") * sec_dev
    first_row = lax.axis_index("tile") * strip
    count = start_modes.shape[0]
    section_ids = (sec_base + jnp.arange(count, dtype=jnp.int32)) % total_sections
    matches = section_ids[:, None] == jnp.arange(total_sections, dtype=jnp.int32)[None, :]
    local_heights = jnp.sum(jnp.where(matches, heights[None, :], 0), 1)
    center, radius, values = chebyshev_terms(DEG)
    inverse = 1.0 / radius
    row_ids = first_row + jnp.arange(strip, dtype=jnp.int32)
    row_mask = (row_ids[None, :] < local_heights[:, None]).astype(jnp.float32)[:, None, :, None]
    field = start_modes.astype(jnp.float32) * row_mask
    wide_perm = extended(permittivity, (("tile", 1),), DEG)
    wide_ids = first_row - DEG + jnp.arange(strip + 2 * DEG, dtype=jnp.int32)
    inside = (wide_ids[None, :] >= 0) & (wide_ids[None, :] < local_heights[:, None])
    wide_mask = inside.astype(jnp.float32)[:, None, :, None]
    wide_diag = (
        (4.0 + SHIFT_DIAG - EPS_WEIGHT * wide_perm.astype(jnp.float32) - center) * inverse
    )[:, None]

    def apply_local(current):
        padded = jnp.pad(current, ((0, 0), (0, 0), (1, 1), (0, 0)))
        return scaled_apply(padded, current, wide_diag, wide_mask, inverse)

    for step in range(STEPS):
        widened = extended(field, (("tile", 2),), DEG)
        field = orthonormal(filter_steps(widened, apply_local, DEG)[:, :, DEG : DEG + strip, :])
    scaled = (field * columns).astype(jnp.bfloat16)
    arriving = passed_along(scaled[:1], "sec", -1)
    following = jnp.concatenate([scaled[1:], arriving], 0)
    local = jnp.einsum("smrc,snrc->smn", scaled, following, preferred_element_type=jnp.float32)
    coupling = lax.psum(local, "tile") / (columns * math.sqrt(columns))
    valid = sec_base + jnp.arange(sec_dev, dtype=jnp.int32) < total_sections - 1
    coupling = jnp.where(valid[:, None, None], coupling, 0.0)
    return (scaled, coupling)


def solution(mesh):
    placed = (P("sec", None, "tile", None), P("sec", "tile", None), P())
    return jax.shard_map(
        per_device,
        mesh=mesh,
        in_specs=placed,
        out_specs=(P("sec", None, "tile", None), P("sec", None, None)),
        check_vma=False,
    )
```

profile of v0, /device:TPU:0, one launch (start us, length us, event | category | flops | bytes accessed | tf_op | source)
XLA Modules:
  0.0 716.3 jit_solution(9335431114228616320)
XLA Ops:
  1.6 2.7 convert_multiply_fusion
  4.4 2.9 copy-done
  7.2 1.6 fusion.135
  8.8 2.5 collective-permute-start.2
  12.6 5.1 collective-permute-start
  19.1 2.9 collective-permute-done.1
  22.2 7.5 %pad_maximum_fusion = f32[8,24,32,384]{3,1,2,0:T(8,128)} fusion(f32[8,24,4,384]{3,1,2,0:T(8,128)S(1)} %collective-permute-done.3, f32[8,24,24,384]{3,1,2,0:T(8,128)} %copy-done, f32[8,24,4,384]{3,1,2,0:T(8,128)S(1)} %collective-permute-done.2), kind=kLoop, calls=%fused_computation.140 | loop fusion | flops 4718592 | bytes 18874368 | tf_op jit(solution)/shard_map/concatenate | solution.py:27
  29.7 21.8 %broadcast_multiply_fusion.2 = (f32[8,24,32,384]{3,1,2,0:T(8,128)}, f32[8,24,32,384]{3,1,2,0:T(8,128)S(1)}) fusion(f32[8,32]{1,0:T(8,128)S(1)} %and_convert_fusion, f32[8,24,32,384]{3,1,2,0:T(8,128)} %pad_maximum_fusion, f32[8,32,384]{2,1,0:T(8,128)S(1)} %get-tuple-element.17), kind=kLoop, calls=%fused_computation.155 | loop fusion | flops 18874368 | bytes 28705792 | tf_op jit(solution)/shard_map/mul | solution.py:56
  51.5 20.3 %fusion.14 = f32[8,24,32,384]{3,1,2,0:T(8,128)} fusion(f32[8,24,32,384]{3,1,2,0:T(8,128)} %get-tuple-element.8, f32[8,24,32,384]{3,1,2,0:T(8,128)S(1)} %get-tuple-element.9, f32[8,32,384]{2,1,0:T(8,128)S(1)} %get-tuple-element.16, f32[8,32]{1,0:T(8,128)S(1)} %and_convert_fusion, f32[8,24,4,384]{3,1,2,0:T(8,128)S(1)} %collective-permute-done.3, ...), kind=kLoop, calls=%fused_computation.63 | loop fusion | flops 28311552 | bytes 38142976 | tf_op jit(solution)/shard_map/sub | solution.py:58
  71.8 22.0 %fusion.22 = f32[8,24,32,384]{3,1,2,0:T(8,128)} fusion(f32[8,24,32,384]{3,1,2,0:T(8,128)} %fusion.14, f32[8,24,32,384]{3,1,2,0:T(8,128)S(1)} %get-tuple-element.9, f32[8,32]{1,0:T(8,128)S(1)} %and_convert_fusion, f32[8,32,384]{2,1,0:T(8,128)S(1)} %get-tuple-element.17), kind=kLoop, calls=%fused_computation.71 | loop fusion | flops 23592960 | bytes 28705792 | tf_op jit(solution)/shard_map/sub | solution.py:58
  93.8 22.0 %fusion.30 = f32[8,24,32,384]{3,1,2,0:T(8,128)S(1)} fusion(f32[8,24,32,384]{3,1,2,0:T(8,128)} %fusion.22, f32[8,24,32,384]{3,1,2,0:T(8,128)} %fusion.14, f32[8,32]{1,0:T(8,128)S(1)} %and_convert_fusion, f32[8,32,384]{2,1,0:T(8,128)S(1)} %get-tuple-element.17), kind=kLoop, calls=%fused_computation.79 | loop fusion | flops 23592960 | bytes 28705792 | tf_op jit(solution)/shard_map/sub | solution.py:58
  115.8 7.4 %fusion.108 = f32[8,24,24]{1,2,0:T(8,128)S(1)} fusion(f32[8,24,32,384]{3,1,2,0:T(8,128)S(1)} %fusion.30), kind=kOutput, calls=%fused_computation.164 | convolution fusion | flops 509607936 | bytes 16533504 | tf_op jit(solution)/shard_map/smrc,snrc->smn/dot_general | solution.py:67
  123.2 3.4 slice_bitcast_fusion.2
  126.6 78.2 %psum.28 = f32[8,24,24]{1,2,0:T(8,128)S(1)} all-reduce(f32[8,24,24]{1,2,0:T(8,128)S(1)} %fusion.108), channel_id=1, replica_groups=mesh['sec'=2,'tile'=16] {'tile'}, use_global_device_ids=true, to_apply=%region_1.2 | all-reduce | flops 4608 | bytes 36864 | tf_op jit(solution)/shard_map/psum | solution.py:68
  204.9 17.6 %custom-call.10 = f32[8,24,24]{2,1,0:T(8,128)S(1)} custom-call(f32[8,24,24]{2,1,0:T(8,128)S(1)} %fusion.126), custom_call_target="Cholesky" | custom-call | tf_op jit(solution)/shard_map/jit(cholesky)/cholesky | solution.py:69
  222.8 14.8 %custom-call.11 = f32[8,1,24,24]{2,3,1,0:T(8,128)S(1)} custom-call(f32[8,1,24,24]{3,2,1,0:T(8,128)S(1)} %select_bitcast_fusion.2), custom_call_target="InvertDiagBlocksLowerTriangular" | custom-call | tf_op jit(solution)/shard_map/triangular_solve/custom-call.0 | solution.py:71
  237.6 3.9 copy.77
  241.5 6.9 fusion.124
  249.0 1.4 collective-permute-start.4
  252.9 1.5 constant_dynamic-update-slice_fusion.1
  255.3 8.6 %broadcast_multiply_fusion.1 = (f32[8,24,32,384]{3,1,2,0:T(8,128)}, f32[8,24,32,384]{3,1,2,0:T(8,128)S(1)}) fusion(f32[8,32]{1,0:T(8,128)S(1)} %and_convert_fusion, f32[8,24,32,384]{3,1,2,0:T(8,128)S(1)} %constant_dynamic-update-slice_fusion, f32[8,32,384]{2,1,0:T(8,128)S(1)} %get-tuple-element.17), kind=kLoop, calls=%fused_computation.154 | loop fusion | flops 18874368 | bytes 28705792 | tf_op jit(solution)/shard_map/mul | solution.py:56
  263.9 18.3 %fusion.44 = f32[8,24,32,384]{3,1,2,0:T(8,128)S(1)} fusion(f32[8,24,32,384]{3,1,2,0:T(8,128)} %get-tuple-element.6, f32[8,24,32,384]{3,1,2,0:T(8,128)} %copy-done.1, f32[8,24,32,384]{3,1,2,0:T(8,128)S(1)} %get-tuple-element.7, f32[8,32,384]{2,1,0:T(8,128)} %copy-done.3, f32[8,32]{1,0:T(8,128)S(1)} %and_convert_fusion), kind=kLoop, calls=%fused_computation.93 | loop fusion | flops 23592960 | bytes 38142976 | tf_op jit(solution)/shard_map/sub | solution.py:58
  282.2 8.5 %fusion.52 = f32[8,24,32,384]{3,1,2,0:T(8,128)} fusion(f32[8,24,32,384]{3,1,2,0:T(8,128)S(1)} %fusion.44, f32[8,24,32,384]{3,1,2,0:T(8,128)S(1)} %get-tuple-element.7, f32[8,32]{1,0:T(8,128)S(1)} %and_convert_fusion, f32[8,32,384]{2,1,0:T(8,128)S(1)} %get-tuple-element.17), kind=kLoop, calls=%fused_computation.101 | loop fusion | flops 23592960 | bytes 28705792 | tf_op jit(solution)/shard_map/sub | solution.py:58
  290.7 21.3 %fusion.60 = f32[8,24,32,384]{3,1,2,0:T(8,128)S(1)} fusion(f32[8,24,32,384]{3,1,2,0:T(8,128)} %fusion.52, f32[8,24,32,384]{3,1,2,0:T(8,128)S(1)} %fusion.44, f32[8,32]{1,0:T(8,128)S(1)} %and_convert_fusion, f32[8,32,384]{2,1,0:T(8,128)S(1)} %get-tuple-element.17), kind=kLoop, calls=%fused_computation.109 | loop fusion | flops 23592960 | bytes 28705792 | tf_op jit(solution)/shard_map/sub | solution.py:58
  312.0 7.4 %fusion.111 = f32[8,24,24]{1,2,0:T(8,128)S(1)} fusion(f32[8,24,32,384]{3,1,2,0:T(8,128)S(1)} %fusion.60), kind=kOutput, calls=%fused_computation.165 | convolution fusion | flops 509607936 | bytes 16533504 | tf_op jit(solution)/shard_map/smrc,snrc->smn/dot_general | solution.py:67
  319.4 3.4 slice_bitcast_fusion.1
  322.8 79.0 %psum.29 = f32[8,24,24]{1,2,0:T(8,128)S(1)} all-reduce(f32[8,24,24]{1,2,0:T(8,128)S(1)} %fusion.111), channel_id=1, replica_groups=mesh['sec'=2,'tile'=16] {'tile'}, use_global_device_ids=true, to_apply=%region_4.7 | all-reduce | flops 4608 | bytes 36864 | tf_op jit(solution)/shard_map/psum | solution.py:68
  401.9 17.6 %custom-call.12 = f32[8,24,24]{2,1,0:T(8,128)S(1)} custom-call(f32[8,24,24]{2,1,0:T(8,128)S(1)} %fusion.123), custom_call_target="Cholesky" | custom-call | tf_op jit(solution)/shard_map/jit(cholesky)/cholesky | solution.py:69
  419.7 14.8 %custom-call.13 = f32[8,1,24,24]{2,3,1,0:T(8,128)S(1)} custom-call(f32[8,1,24,24]{3,2,1,0:T(8,128)S(1)} %select_bitcast_fusion.1), custom_call_target="InvertDiagBlocksLowerTriangular" | custom-call | tf_op jit(solution)/shard_map/triangular_solve/custom-call.0 | solution.py:71
  434.6 3.9 copy.78
  438.4 6.9 fusion.121
  446.0 1.4 collective-permute-start.6
  452.2 8.6 %broadcast_multiply_fusion = (f32[8,24,32,384]{3,1,2,0:T(8,128)}, f32[8,24,32,384]{3,1,2,0:T(8,128)S(1)}) fusion(f32[8,32]{1,0:T(8,128)S(1)} %and_convert_fusion, f32[8,24,32,384]{3,1,2,0:T(8,128)S(1)} %constant_dynamic-update-slice_fusion.3, f32[8,32,384]{2,1,0:T(8,128)S(1)} %get-tuple-element.17), kind=kLoop, calls=%fused_computation.153 | loop fusion | flops 18874368 | bytes 28705792 | tf_op jit(solution)/shard_map/mul | solution.py:56
  460.9 18.3 %fusion.74 = f32[8,24,32,384]{3,1,2,0:T(8,128)S(1)} fusion(f32[8,24,32,384]{3,1,2,0:T(8,128)} %get-tuple-element.4, f32[8,24,32,384]{3,1,2,0:T(8,128)} %copy-done.2, f32[8,24,32,384]{3,1,2,0:T(8,128)S(1)} %get-tuple-element.5, f32[8,32,384]{2,1,0:T(8,128)} %copy-done.3, f32[8,32]{1,0:T(8,128)S(1)} %and_convert_fusion), kind=kLoop, calls=%fused_computation.123 | loop fusion | flops 23592960 | bytes 38142976 | tf_op jit(solution)/shard_map/sub | solution.py:58
  479.1 8.5 %fusion.82 = f32[8,24,32,384]{3,1,2,0:T(8,128)} fusion(f32[8,24,32,384]{3,1,2,0:T(8,128)S(1)} %fusion.74, f32[8,24,32,384]{3,1,2,0:T(8,128)S(1)} %get-tuple-element.5, f32[8,32]{1,0:T(8,128)S(1)} %and_convert_fusion, f32[8,32,384]{2,1,0:T(8,128)S(1)} %get-tuple-element.17), kind=kLoop, calls=%fused_computation.131 | loop fusion | flops 23592960 | bytes 28705792 | tf_op jit(solution)/shard_map/sub | solution.py:58
  487.7 21.6 %fusion.90 = f32[8,24,32,384]{3,1,2,0:T(8,128)S(1)} fusion(f32[8,24,32,384]{3,1,2,0:T(8,128)} %fusion.82, f32[8,24,32,384]{3,1,2,0:T(8,128)S(1)} %fusion.74, f32[8,32]{1,0:T(8,128)S(1)} %and_convert_fusion, f32[8,32,384]{2,1,0:T(8,128)S(1)} %get-tuple-element.17), kind=kLoop, calls=%fused_computation.139 | loop fusion | flops 23592960 | bytes 28705792 | tf_op jit(solution)/shard_map/sub | solution.py:58
  509.2 7.4 %fusion.114 = f32[8,24,24]{1,2,0:T(8,128)S(1)} fusion(f32[8,24,32,384]{3,1,2,0:T(8,128)S(1)} %fusion.90), kind=kOutput, calls=%fused_computation.166 | convolution fusion | flops 509607936 | bytes 16533504 | tf_op jit(solution)/shard_map/smrc,snrc->smn/dot_general | solution.py:67
  516.7 3.4 slice_bitcast_fusion
  520.1 78.4 %psum.30 = f32[8,24,24]{1,2,0:T(8,128)S(1)} all-reduce(f32[8,24,24]{1,2,0:T(8,128)S(1)} %fusion.114), channel_id=1, replica_groups=mesh['sec'=2,'tile'=16] {'tile'}, use_global_device_ids=true, to_apply=%region_5.8 | all-reduce | flops 4608 | bytes 36864 | tf_op jit(solution)/shard_map/psum | solution.py:68
  598.6 17.6 %custom-call.14 = f32[8,24,24]{2,1,0:T(8,128)S(1)} custom-call(f32[8,24,24]{2,1,0:T(8,128)S(1)} %fusion.120), custom_call_target="Cholesky" | custom-call | tf_op jit(solution)/shard_map/jit(cholesky)/cholesky | solution.py:69
  616.5 14.8 %custom-call.15 = f32[8,1,24,24]{2,3,1,0:T(8,128)S(1)} custom-call(f32[8,1,24,24]{3,2,1,0:T(8,128)S(1)} %select_bitcast_fusion), custom_call_target="InvertDiagBlocksLowerTriangular" | custom-call | tf_op jit(solution)/shard_map/triangular_solve/custom-call.0 | solution.py:71
  631.3 3.9 copy.79
  635.1 6.5 fusion
  641.8 1.5 collective-permute-start.8
  643.9 2.5 copy.80
  646.4 5.6 collective-permute-done.8
  652.0 1.4 fusion.103
  653.3 62.0 %psum.31 = f32[8,24,24]{2,1,0:T(8,128)S(1)} all-reduce(f32[8,24,24]{2,1,0:T(8,128)S(1)} %fusion.103), channel_id=1, replica_groups=mesh['sec'=2,'tile'=16] {'tile'}, use_global_device_ids=true, to_apply=%region_6.9 | all-reduce | flops 4608 | bytes 36864 | tf_op jit(solution)/shard_map/psum | solution.py:110
  (61 shorter events, 15.5 us)
Async XLA Ops:
  0.6 11.9 %copy-start.4 = (bf16[8,24,384]{2,1,0:T(8,128)(2,1)S(1)}, bf16[8,24,384]{2,1,0:T(8,128)(2,1)}, u32[]{:S(2)}) copy-start(bf16[8,24,384]{2,1,0:T(8,128)(2,1)} %param.7) | copy-start | bytes 442372
  4.3 2.9 copy-start
  8.8 13.4 %collective-permute-start.2 = (f32[8,24,4,384]{3,1,2,0:T(8,128)}, f32[8,24,4,384]{3,1,2,0:T(8,128)S(1)}, u32[]{:S(2)}, u32[]{:S(2)}) collective-permute-start(f32[8,24,4,384]{3,1,2,0:T(8,128)} %get-tuple-element.14), channel_id=1, source_target_pairs={{0,1},{1,2},{2,3},{3,4},{4,5},{5,6},{6,7},{7,8},{8,9},{9,10},{10,1... | collective-permute-start | bytes 3538952 | tf_op jit(solution)/shard_map/ppermute | solution.py:25
  11.3 10.9 %collective-permute-start.3 = (f32[8,24,4,384]{3,1,2,0:T(8,128)}, f32[8,24,4,384]{3,1,2,0:T(8,128)S(1)}, u32[]{:S(2)}, u32[]{:S(2)}) collective-permute-start(f32[8,24,4,384]{3,1,2,0:T(8,128)} %get-tuple-element.15), channel_id=1, source_target_pairs={{1,0},{2,1},{3,2},{4,3},{5,4},{6,5},{7,6},{8,7},{9,8},{10,9},{11,1... | collective-permute-start | bytes 3538952 | tf_op jit(solution)/shard_map/ppermute | solution.py:26
  12.6 6.5 collective-permute-start
  17.7 4.3 collective-permute-start.1
  22.1 29.4 %copy-start.3 = (f32[8,32,384]{2,1,0:T(8,128)}, f32[8,32,384]{2,1,0:T(8,128)S(1)}, u32[]{:S(2)}) copy-start(f32[8,32,384]{2,1,0:T(8,128)S(1)} %get-tuple-element.16) | copy-start | bytes 1179652
  249.0 3.8 collective-permute-start.4
  250.4 4.7 collective-permute-start.5
  255.3 8.6 %copy-start.1 = (f32[8,24,32,384]{3,1,2,0:T(8,128)}, f32[8,24,32,384]{3,1,2,0:T(8,128)S(1)}, u32[]{:S(2)}) copy-start(f32[8,24,32,384]{3,1,2,0:T(8,128)S(1)} %constant_dynamic-update-slice_fusion) | copy-start | bytes 28311556
  446.0 3.8 collective-permute-start.6
  447.4 4.7 collective-permute-start.7
  452.2 8.6 %copy-start.2 = (f32[8,24,32,384]{3,1,2,0:T(8,128)}, f32[8,24,32,384]{3,1,2,0:T(8,128)S(1)}, u32[]{:S(2)}) copy-start(f32[8,24,32,384]{3,1,2,0:T(8,128)S(1)} %constant_dynamic-update-slice_fusion.3) | copy-start | bytes 28311556
  641.8 10.2 %collective-permute-start.8 = (bf16[1,24,24,384]{3,1,2,0:T(8,128)(2,1)S(1)}, bf16[1,24,24,384]{3,1,2,0:T(8,128)(2,1)S(1)}, u32[]{:S(2)}, u32[]{:S(2)}) collective-permute-start(bf16[1,24,24,384]{3,1,2,0:T(8,128)(2,1)S(1)} %bitcast.96), channel_id=1, source_target_pairs={{16,0},{17,1},{18,2},{19,3},{20,4},{21,5},{22,6},{23,7},{24,8},{25... | collective-permute-start | bytes 1327112 | tf_op jit(solution)/shard_map/ppermute | solution.py:34
where the time goes:
time: 723 us; the launch traced here: 716 us
  other arithmetic  310 us (43%)
  blocking collectives  298 us (41%)
  matrix products  43.9 us (6%)
  local copies, waits for them, and re-layouts  34.1 us (5%)
  starting transfers between devices  16.9 us (2%)
  waiting for transfers between devices  12.5 us (2%)
    psum x3, blocking collectives, orthonormal(): gram = lax.psum(local, 'tile')  236 us
    sub x9, other arithmetic, filter_steps(): apply_once(current) * (2.0 * values[order] / values[order + 1])  161 us
    psum x1, blocking collectives, per_device(): coupling = lax.psum(local, 'tile') / (columns * math.sqrt(columns))  62 us
    another operation x10, other arithmetic, orthonormal(): lower = jnp.linalg.cholesky(gram)  53.3 us
    another operation x7, other arithmetic, orthonormal(): lax.linalg.triangular_solve(lower, flat, left_side=True, lower=True)  44.7 us
    mul x3, other arithmetic, filter_steps(): current = apply_once(field) * (1.0 / values[1])  39.1 us
    dot_general x3, matrix products, orthonormal(): jnp.einsum('smrc,snrc->smn', field, field, precision=lax.Precision.HIGHEST)  22.2 us
    another operation x3, matrix products, orthonormal(): lax.linalg.triangular_solve(lower, flat, left_side=True, lower=True)  20.3 us
  transfers between devices with their start and end apart: 9, of which 6 were waited for; matrix products, arithmetic and copies ran while one was open for 1% of the time, Pallas kernels for 0%

commit v1 on v0

v1 whole, which is shorter than its diff:
```python
import functools
import math

import jax
import jax.numpy as jnp
from jax import lax
from jax.experimental import pallas as pl
from jax.experimental.pallas import tpu as pltpu
from jax.sharding import PartitionSpec as P

STEPS = 3
DEG = 4
SHIFT_DIAG = 3.0
EPS_WEIGHT = 0.25
LOWER_EDGE = 2.0
UPPER_EDGE = 10.75
CENTER = 0.5 * (UPPER_EDGE + LOWER_EDGE)
RADIUS = 0.5 * (UPPER_EDGE - LOWER_EDGE)
LANES = 128
SLOT = 32
PER = LANES // SLOT
BLOCK = 4
NT = (((1,), (1,)), ((), ()))
MESH = pl.DeviceIdType.MESH


def iota(shape, dim):
    return lax.broadcasted_iota(jnp.int32, shape, dim)


def dot32(a, b):
    return jnp.dot(a, b, preferred_element_type=jnp.float32)


def dot_nt(a, b):
    return lax.dot_general(a, b, NT, preferred_element_type=jnp.float32)


def halo(x, dim, width):
    size, strip = lax.axis_size("tile"), x.shape[dim]
    above, below = [], []
    for hop in range(1, -(-width // strip) + 1):
        rows = min(strip, width - (hop - 1) * strip)
        last = lax.slice_in_dim(x, strip - rows, strip, axis=dim)
        first = lax.slice_in_dim(x, 0, rows, axis=dim)
        above.insert(0, lax.ppermute(last, "tile", [(i, i + hop) for i in range(size - hop)]))
        below.append(lax.ppermute(first, "tile", [(i + hop, i) for i in range(size - hop)]))
    return above, below


def widened(x, dim, width, total):
    above, below = halo(x, dim, width)
    spare = total - x.shape[dim] - 2 * width
    parts = above + [x] + below
    if spare:
        shape = list(x.shape)
        shape[dim] = spare
        parts.append(jnp.zeros(shape, x.dtype))
    return jnp.concatenate(parts, axis=dim)


def interleave(columns, groups, inverse=False):
    row, col = iota((columns, columns), 0), iota((columns, columns), 1)
    if inverse:
        row, col = col, row
    return (row == groups * (col % LANES) + col // LANES).astype(jnp.bfloat16)


def place(small, wide_ref, out_ref, s, modes):
    wide_ref[:, 0:modes] = small
    moved = pltpu.roll(wide_ref[...], SLOT * lax.rem(s, PER), 1)
    group = s // PER
    out_ref[group] = out_ref[group] + moved


def filter_kernel(strip, heights, x_ref, perm_ref, field_ref, gram_ref, a_ref, b_ref, q_ref, mix_ref, high_ref, low_ref, wide_ref):
    modes, rows, columns = x_ref.shape[1:]
    groups = columns // LANES
    width = STEPS * DEG
    used = strip + 2 * width
    s = pl.program_id(0)
    sections = pl.num_programs(0)
    height = heights[lax.axis_index("sec") * sections + s]
    top = lax.axis_index("tile") * strip - width

    @pl.when(s == 0)
    def _():
        mix_ref[...] = interleave(columns, groups)
        a_ref[...] = jnp.zeros_like(a_ref)
        b_ref[...] = jnp.zeros_like(b_ref)
        wide_ref[...] = jnp.zeros_like(wide_ref)
        gram_ref[...] = jnp.zeros_like(gram_ref)

    mix = mix_ref[...]
    row_ids = top + iota((rows, LANES), 0)
    valid = (row_ids >= 0) & (row_ids < height)
    batch = 4
    for m0 in range(0, modes, batch):
        moved = dot32(x_ref[0, m0 : m0 + batch].reshape(batch * rows, columns), mix)
        for m in range(batch):
            for j in range(groups):
                value = moved[m * rows : (m + 1) * rows, j * LANES : (j + 1) * LANES]
                a_ref[j, pl.ds(modes + m0 + m, rows, stride=modes), :] = jnp.where(valid, value, 0.0)
    perm = dot32(perm_ref[0], mix)
    diag = (4.0 + SHIFT_DIAG - EPS_WEIGHT * perm - CENTER) * (2.0 / RADIUS)
    for j in range(groups):
        q_ref[j] = diag[:, j * LANES : (j + 1) * LANES]

    lane = iota((8, LANES), 1)
    is_first, is_last = lane == 0, lane == LANES - 1

    def stage(src, dst, order, start):
        low = BLOCK * (order // BLOCK)
        blocks = -(-(used - order - low) // BLOCK)

        def body(block, carry):
            row0 = low + block * BLOCK
            base = pl.multiple_of((row0 + 1) * modes, 8)
            for tile in range(modes // 8):
                def load(ref, i, j):
                    return ref[j, pl.ds(pl.multiple_of(base + (i * modes + tile * 8), 8), 8), :]

                before = [load(src, -1, j) for j in range(groups)]
                here = [load(src, 0, j) for j in range(groups)]
                for i in range(BLOCK):
                    after = [load(src, i + 1, j) for j in range(groups)]
                    row = top + row0 + i
                    inside = (row >= 0) & (row < height)
                    weight = jnp.where(inside, 2.0 / RADIUS, 0.0).astype(jnp.float32)
                    left = jnp.where(is_first, 0.0, pltpu.roll(here[groups - 1], 1, 1))
                    right = jnp.where(is_last, 0.0, pltpu.roll(here[0], LANES - 1, 1))
                    for j in range(groups):
                        side = (here[j - 1] if j else left) + (here[j + 1] if j < groups - 1 else right)
                        beside = (before[j] + after[j]) + side
                        q = jnp.broadcast_to(q_ref[j, pl.ds(row0 + i, 1), :], (8, LANES))
                        value = q * here[j] - weight * beside
                        if start:
                            value = 0.5 * value
                        else:
                            value = value - load(dst, i, j)
                        dst[j, pl.ds(pl.multiple_of(base + (i * modes + tile * 8), 8), 8), :] = value
                    before, here = here, after
            return carry

        lax.fori_loop(0, blocks, body, 0)

    for step in range(STEPS):
        for k in range(DEG):
            src, dst = (a_ref, b_ref) if k % 2 == 0 else (b_ref, a_ref)
            stage(src, dst, step * DEG + k + 1, k == 0)

    for j in range(groups):
        field_ref[0, j] = a_ref[j, (width + 1) * modes : (width + 1 + strip) * modes, :]
    for r in range(strip):
        for j in range(groups):
            value = a_ref[j, (width + 1 + r) * modes : (width + 2 + r) * modes, :]
            high = value.astype(jnp.bfloat16)
            place_at = slice((r * groups + j) * LANES, (r * groups + j + 1) * LANES)
            high_ref[:, place_at] = high
            low_ref[:, place_at] = (value - high.astype(jnp.float32)).astype(jnp.bfloat16)
    high, low = high_ref[...], low_ref[...]
    gram = dot_nt(high, high) + (dot_nt(high, low) + dot_nt(low, high))
    place(gram, wide_ref, gram_ref, s, modes)


def gathered_sum(x_ref, slots, send_sem, recv_sem):
    count = lax.axis_size("tile")
    me = lax.axis_index("tile")
    barrier = pltpu.get_barrier_semaphore()

    def greet(d, carry):
        pl.semaphore_signal(barrier, inc=1, device_id={"tile": lax.rem(me + d, count)}, device_id_type=MESH)
        return carry

    lax.fori_loop(1, count, greet, 0)
    pl.semaphore_wait(barrier, count - 1)

    def copy_to(d, slot):
        return pltpu.make_async_remote_copy(
            src_ref=x_ref,
            dst_ref=slots.at[slot],
            send_sem=send_sem.at[d],
            recv_sem=recv_sem.at[slot],
            device_id={"tile": lax.rem(me + d, count)},
            device_id_type=MESH,
        )

    def send(d, carry):
        copy_to(d, me).start()
        return carry

    def finish(d, carry):
        copy_to(d, lax.rem(me + count - d, count)).wait_recv()
        copy_to(d, me).wait_send()
        return carry

    lax.fori_loop(1, count, send, 0)
    slots[me] = x_ref[...]
    lax.fori_loop(1, count, finish, 0)
    return lax.fori_loop(1, count, lambda i, total: total + slots[i], slots[0])


def spread(total, sections):
    return jnp.stack([pltpu.roll(total[s // PER], (LANES - SLOT * (s % PER)) % LANES, 1) if s % PER else total[s // PER] for s in range(sections)])


def factor_kernel(scale, x_ref, out_ref, slots, send_sem, recv_sem):
    sections, modes, _ = out_ref.shape
    total = gathered_sum(x_ref, slots, send_sem, recv_sem)
    shape = (sections, modes, LANES)
    row, lane = iota(shape, 1), iota(shape, 2)
    work = jnp.where(lane < modes, spread(total, sections), jnp.where(lane == row + SLOT, 1.0, 0.0))
    for k in range(modes):
        top = work[:, k : k + 1, :]
        pivot = jnp.sqrt(work[:, k : k + 1, k : k + 1])
        top = top / pivot
        column = work[:, :, k : k + 1] / pivot
        work = jnp.where(row > k, work - column * top, jnp.where(row == k, top, work))
    for s in range(sections):
        moved = pltpu.roll(work[s], LANES - SLOT, 1)
        out_ref[s] = moved[:, 0:modes] * scale


def apply_kernel(strip, inv_ref, field_ref, out_ref, first_ref, last_ref, pack_ref, unmix_ref, both_ref, rows_ref, wide_ref):
    modes = inv_ref.shape[1]
    groups = field_ref.shape[1]
    columns = groups * LANES
    s = pl.program_id(0)
    take = max(n for n in range(1, 9) if strip % n == 0)
    size = take * modes

    @pl.when(s == 0)
    def _():
        unmix_ref[...] = interleave(columns, groups, True)
        wide_ref[...] = jnp.zeros_like(wide_ref)
        pack_ref[...] = jnp.zeros_like(pack_ref)

    copies = (iota((size, modes), 0) % modes == iota((size, modes), 1)).astype(jnp.bfloat16)
    same = iota((size, size), 0) // modes == iota((size, size), 1) // modes

    def block_diagonal(part):
        tall = dot32(copies, part).astype(jnp.bfloat16)
        return jnp.where(same, dot_nt(tall, copies), 0.0).astype(jnp.bfloat16)

    inv = inv_ref[0]
    inv_high = inv.astype(jnp.bfloat16)
    inv_low = (inv - inv_high.astype(jnp.float32)).astype(jnp.bfloat16)
    left_high, left_low = block_diagonal(inv_high), block_diagonal(inv_low)
    unmix = unmix_ref[...]
    slot = lax.rem(s, 2)
    for r0 in range(0, strip, take):
        value = jnp.concatenate([field_ref[0, j, r0 * modes : r0 * modes + size, :] for j in range(groups)], axis=1)
        high = value.astype(jnp.bfloat16)
        low = (value - high.astype(jnp.float32)).astype(jnp.bfloat16)
        solved = dot32(left_high, high) + (dot32(left_low, high) + dot32(left_high, low))
        for r in range(take):
            both_ref[slot, :, (r0 + r) * columns : (r0 + r + 1) * columns] = solved[r * modes : (r + 1) * modes].astype(jnp.bfloat16)
        natural = dot32(solved.astype(jnp.bfloat16), unmix)
        for j in range(groups):
            rows_ref[j, r0 * modes : r0 * modes + size, :] = natural[:, j * LANES : (j + 1) * LANES]
    for m in range(modes):
        for j in range(groups):
            out_ref[0, m, :, j * LANES : (j + 1) * LANES] = rows_ref[j, pl.ds(m, strip, stride=modes), :].astype(jnp.bfloat16)

    @pl.when(s == 0)
    def _():
        first_ref[...] = both_ref[slot]

    @pl.when(s > 0)
    def _():
        place(dot_nt(both_ref[1 - slot], both_ref[slot]), wide_ref, pack_ref, s - 1, modes)

    @pl.when(s == pl.num_programs(0) - 1)
    def _():
        last_ref[...] = both_ref[slot]


def edge_kernel(sections, pack_ref, last_ref, next_ref, out_ref, wide_ref):
    wide_ref[...] = jnp.zeros_like(wide_ref)
    out_ref[...] = pack_ref[...]
    place(dot_nt(last_ref[...], next_ref[...]), wide_ref, out_ref, jnp.int32(sections - 1), last_ref.shape[0])


def couple_kernel(columns, x_ref, out_ref, slots, send_sem, recv_sem):
    sections, modes, _ = out_ref.shape
    total = gathered_sum(x_ref, slots, send_sem, recv_sem)
    parts = spread(total, sections)
    end = lax.axis_size("sec") * sections - 1
    for s in range(sections):
        kept = jnp.where(lax.axis_index("sec") * sections + s < end, 1.0 / (columns * math.sqrt(columns)), 0.0)
        out_ref[s] = parts[s][:, 0:modes] * kept.astype(jnp.float32)


def per_device(start_modes, permittivity, heights):
    sections, modes, strip, columns = start_modes.shape
    groups = columns // LANES
    width = STEPS * DEG
    rows = -(-(strip + 2 * width) // 16) * 16
    packs = -(-sections // PER)
    tiles = lax.axis_size("tile")
    f32, bf16 = jnp.float32, jnp.bfloat16
    x = widened(start_modes, 2, width, rows)
    perm = widened(permittivity, 1, width, rows)
    pack_shape = jax.ShapeDtypeStruct((packs, modes, LANES), f32)
    pack_spec = pl.BlockSpec((packs, modes, LANES), lambda s, *_: (0, 0, 0))
    field_spec = pl.BlockSpec((1, groups, strip * modes, LANES), lambda s, *_: (s, 0, 0, 0))
    field, gram = pl.pallas_call(
        functools.partial(filter_kernel, strip),
        grid_spec=pltpu.PrefetchScalarGridSpec(
            num_scalar_prefetch=1,
            grid=(sections,),
            in_specs=[
                pl.BlockSpec((1, modes, rows, columns), lambda s, *_: (s, 0, 0, 0)),
                pl.BlockSpec((1, rows, columns), lambda s, *_: (s, 0, 0)),
            ],
            out_specs=[field_spec, pack_spec],
            scratch_shapes=[
                pltpu.VMEM((groups, (rows + 2) * modes, LANES), f32),
                pltpu.VMEM((groups, (rows + 2) * modes, LANES), f32),
                pltpu.VMEM((groups, rows, LANES), f32),
                pltpu.VMEM((columns, columns), bf16),
                pltpu.VMEM((modes, strip * columns), bf16),
                pltpu.VMEM((modes, strip * columns), bf16),
                pltpu.VMEM((modes, LANES), f32),
            ],
        ),
        out_shape=[jax.ShapeDtypeStruct((sections, groups, strip * modes, LANES), f32), pack_shape],
        name="filter",
    )(heights, x, perm)

    def exchanged(kernel, value, collective_id, name):
        return pl.pallas_call(
            kernel,
            out_shape=jax.ShapeDtypeStruct((sections, modes, modes), f32),
            in_specs=[pl.BlockSpec(memory_space=pltpu.VMEM)],
            out_specs=pl.BlockSpec(memory_space=pltpu.VMEM),
            scratch_shapes=[
                pltpu.VMEM((tiles, packs, modes, LANES), f32),
                pltpu.SemaphoreType.DMA((tiles,)),
                pltpu.SemaphoreType.DMA((tiles,)),
            ],
            compiler_params=pltpu.CompilerParams(collective_id=collective_id, has_side_effects=True),
            name=name,
        )(value)

    inverse = exchanged(functools.partial(factor_kernel, float(columns)), gram, 0, "factor")
    flat = jax.ShapeDtypeStruct((modes, strip * columns), bf16)
    flat_spec = pl.BlockSpec((modes, strip * columns), lambda s: (0, 0))
    scaled, first, last, pack = pl.pallas_call(
        functools.partial(apply_kernel, strip),
        grid=(sections,),
        in_specs=[pl.BlockSpec((1, modes, modes), lambda s: (s, 0, 0)), field_spec],
        out_specs=[pl.BlockSpec((1, modes, strip, columns), lambda s: (s, 0, 0, 0)), flat_spec, flat_spec, pack_spec],
        out_shape=[jax.ShapeDtypeStruct((sections, modes, strip, columns), bf16), flat, flat, pack_shape],
        scratch_shapes=[
            pltpu.VMEM((columns, columns), bf16),
            pltpu.VMEM((2, modes, strip * columns), bf16),
            pltpu.VMEM((groups, strip * modes, LANES), f32),
            pltpu.VMEM((modes, LANES), f32),
        ],
        name="apply",
    )(inverse, field)
    count = lax.axis_size("sec")
    arriving = lax.ppermute(first, "sec", [(i + 1, i) for i in range(count - 1)])
    pack = pl.pallas_call(
        functools.partial(edge_kernel, sections),
        out_shape=pack_shape,
        scratch_shapes=[pltpu.VMEM((modes, LANES), f32)],
        name="edge",
    )(pack, last, arriving)
    coupling = exchanged(functools.partial(couple_kernel, columns), pack, 1, "couple")
    return (scaled, coupling)


def solution(mesh):
    placed = (P("sec", None, "tile", None), P("sec", "tile", None), P())
    return jax.shard_map(
        per_device,
        mesh=mesh,
        in_specs=placed,
        out_specs=(P("sec", None, "tile", None), P("sec", None, None)),
        check_vma=False,
    )
```

time: 723 us -> 241 us (0.33)
  other arithmetic: 310 us -> 5.8 us
  blocking collectives: 298 us -> 0 us
  Pallas kernels: 0 us -> 198 us
  matrix products: 43.9 us -> 0 us
  local copies, waits for them, and re-layouts: 34.1 us -> 8.53 us
    psum x4 -> x0, blocking collectives: 298 us -> none  [the longest x3 236 us: orthonormal(): gram = lax.psum(local, 'tile')]
    pallas_call x0 -> x5, Pallas kernels: none -> 198 us  [the longest x1 115 us: per_device(): pl.pallas_call(functools.partial(filter_kernel, strip), grid_spec=pltpu.P...]
    sub x9 -> x0, other arithmetic: 161 us -> none  [filter_steps(): apply_once(current) * (2.0 * values[order] / values[order + 1])]
    another operation x17 -> x0, other arithmetic: 98 us -> none  [the longest x10 53.3 us: orthonormal(): lower = jnp.linalg.cholesky(gram)]
    mul x5 -> x0, other arithmetic: 41.9 us -> none  [the longest x3 39.1 us: filter_steps(): current = apply_once(field) * (1.0 / values[1])]
    dot_general x4 -> x0, matrix products: 23.6 us -> none  [the longest x3 22.2 us: orthonormal(): jnp.einsum('smrc,snrc->smn', field, field, precision=lax.Precision.HIGHEST)]
    another operation x3 -> x0, matrix products: 20.3 us -> none  [orthonormal(): lax.linalg.triangular_solve(lower, flat, left_side=True, lower=True)]
    unnamed x18 -> x9, local copies, waits for them, and re-layouts: 18.6 us -> 4.3 us
  transfers between devices with their start and end apart: 9 -> 5, of which waited for: 6 -> 2; matrix products, arithmetic and copies ran while one was open for 1% -> 1% of each run, Pallas kernels for 0% -> 0%
where the time goes in v1:
time: 241 us; the launch traced here: 240 us
  Pallas kernels  198 us (82%)
  waiting for transfers between devices  15.2 us (6%)
  starting transfers between devices  11.4 us (5%)
  local copies, waits for them, and re-layouts  8.53 us (4%)
  other arithmetic  5.8 us (2%)
    pallas_call x1, Pallas kernels, per_device(): pl.pallas_call(functools.partial(filter_kernel, strip), grid_spec=pltpu.P...  115 us
    pallas_call x2, Pallas kernels, exchanged(): pl.pallas_call(kernel, out_shape=jax.ShapeDtypeStruct((sections, modes, m...  63.9 us
    pallas_call x1, Pallas kernels, per_device(): pl.pallas_call(functools.partial(apply_kernel, strip), grid=(sections,),...  16.8 us
    ppermute x1, waiting for transfers between devices, per_device(): lax.ppermute(first, 'sec', [(i + 1, i) for i in range(count - 1)])  13.3 us
    ppermute x2, starting transfers between devices, halo(): lax.ppermute(last, 'tile', [(i, i + hop) for i in range(size - hop)])  7.56 us
    concatenate x2, other arithmetic, widened(): return jnp.concatenate(parts, axis=dim)  5.8 us
  transfers between devices with their start and end apart: 5, of which 2 were waited for; matrix products, arithmetic and copies ran while one was open for 1% of the time, Pallas kernels for 0%

profile of v1, /device:TPU:0, one launch (start us, length us, event | category | flops | bytes accessed | tf_op | source)
XLA Modules:
  0.0 239.6 jit_solution(7998149898701685186)
XLA Ops:
  0.6 3.4 %fusion = (bf16[8,24,12,384]{3,2,1,0:T(8,128)(2,1)S(1)}, bf16[8,24,12,384]{3,2,1,0:T(8,128)(2,1)S(1)}) fusion(bf16[8,24,24,384]{3,2,1,0:T(8,128)(2,1)} %param.3), kind=kLoop, calls=%fused_computation.2 | loop fusion | bytes 7077888 | tf_op jit(solution)/shard_map/slice | solution.py:44
  4.1 0.0 copy-start.1
  4.1 0.4 copy.10
  4.5 1.3 collective-permute-start.1
  5.8 0.4 copy.9
  6.2 3.1 %collective-permute-start = (bf16[8,24,12,384]{3,1,2,0:T(8,128)(2,1)S(1)}, bf16[8,24,12,384]{3,1,2,0:T(8,128)(2,1)S(1)}, u32[]{:S(2)}, u32[]{:S(2)}) collective-permute-start(bf16[8,24,12,384]{3,1,2,0:T(8,128)(2,1)S(1)} %copy.9), channel_id=1, source_target_pairs={{0,1},{1,2},{2,3},{3,4},{4,5},{5,6},{6,7},{7,8},{8,9},{9,10},{10,1... | collective-permute-start | bytes 5308424 | tf_op jit(solution)/shard_map/ppermute | solution.py:46
  9.3 0.0 copy-done.1
  9.4 4.4 %collective-permute-start.2 = (bf16[8,12,384]{2,1,0:T(8,128)(2,1)S(1)}, bf16[8,12,384]{2,1,0:T(8,128)(2,1)S(1)}, u32[]{:S(2)}, u32[]{:S(2)}) collective-permute-start(bf16[8,12,384]{2,1,0:T(8,128)(2,1)S(1)} %get-tuple-element.16), channel_id=1, source_target_pairs={{0,1},{1,2},{2,3},{3,4},{4,5},{5,6},{6,7},{7,8},{8,9},{9,10},{10,1... | collective-permute-start | bytes 221192 | tf_op jit(solution)/shard_map/ppermute | solution.py:46
  13.8 1.3 collective-permute-start.3
  15.1 0.0 collective-permute-done.2
  15.1 1.9 collective-permute-done.3
  17.0 0.8 pad_maximum_fusion.1.perm_ref
  17.8 0.0 copy-start
  17.8 0.0 collective-permute-done.1
  17.8 0.4 copy.8
  18.2 0.0 collective-permute-done
  18.2 0.4 copy.7
  18.6 1.2 copy-done
  19.8 5.0 %pad_maximum_fusion.x_ref = bf16[8,24,48,384]{3,2,1,0:T(8,128)(2,1)} fusion(bf16[8,24,12,384]{3,2,1,0:T(8,128)(2,1)S(1)} %copy.8, bf16[8,24,24,384]{3,2,1,0:T(8,128)(2,1)S(1)} %copy-done, bf16[8,24,12,384]{3,2,1,0:T(8,128)(2,1)S(1)} %copy.7), kind=kLoop, calls=%fused_computation | loop fusion | flops 21233664 | bytes 14155776 | tf_op jit(solution)/shard_map/concatenate | solution.py:59
  24.8 115.2 %filter.1 = (f32[8,3,576,128]{3,2,1,0:T(8,128)}, f32[2,24,128]{2,1,0:T(8,128)}) custom-call(s32[16]{0:T(128)} %heights.1, bf16[8,24,48,384]{3,2,1,0:T(8,128)(2,1)} %pad_maximum_fusion.x_ref, bf16[8,48,384]{2,1,0:T(8,128)(2,1)} %pad_maximum_fusion.1.perm_ref), custom_call_target="tpu_custom_call" | custom-call | tf_op jit(solution)/shard_map/filter/pallas_call | solution.py:307
  140.0 49.4 %factor.1.inv_ref = f32[8,24,24]{2,1,0:T(8,128)} custom-call(f32[2,24,128]{2,1,0:T(8,128)} %get-tuple-element.8.x_ref), custom_call_target="tpu_custom_call" | custom-call | tf_op jit(solution)/shard_map/factor/pallas_call | solution.py:332
  189.3 16.8 %apply.1 = (bf16[8,24,24,384]{3,2,1,0:T(8,128)(2,1)}, bf16[24,9216]{1,0:T(8,128)(2,1)}, bf16[24,9216]{1,0:T(8,128)(2,1)}, f32[2,24,128]{2,1,0:T(8,128)}) custom-call(f32[8,24,24]{2,1,0:T(8,128)} %factor.1.inv_ref, f32[8,3,576,128]{3,2,1,0:T(8,128)} %get-tuple-element.9.field_ref), custom_call_target="tpu_custom_call" | custom-call | tf_op jit(solution)/shard_map/apply/pallas_call | solution.py:349
  206.1 1.3 collective-permute-start.4
  207.4 13.3 %collective-permute-done.4.next_ref = bf16[24,9216]{1,0:T(8,128)(2,1)S(1)} collective-permute-done((bf16[24,9216]{1,0:T(8,128)(2,1)}, bf16[24,9216]{1,0:T(8,128)(2,1)S(1)}, u32[]{:S(2)}, u32[]{:S(2)}) %collective-permute-start.4) | collective-permute-done | bytes 442400 | tf_op jit(solution)/shard_map/ppermute | solution.py:364
  220.7 0.0 copy-start.2
  220.7 0.8 copy-done.2
  221.5 2.1 edge.1.x_ref
  223.6 14.5 %couple.1 = f32[8,24,24]{2,1,0:T(8,128)} custom-call(f32[2,24,128]{2,1,0:T(8,128)} %edge.1.x_ref), custom_call_target="tpu_custom_call" | custom-call | tf_op jit(solution)/shard_map/couple/pallas_call | solution.py:332
  238.1 1.5 copy.12
  (1 shorter events, 0.0 us)
Async XLA Ops:
  4.1 5.3 %copy-start.1 = (bf16[8,24,384]{2,1,0:T(8,128)(2,1)S(1)}, bf16[8,24,384]{2,1,0:T(8,128)(2,1)}, u32[]{:S(2)}) copy-start(bf16[8,24,384]{2,1,0:T(8,128)(2,1)} %param.4) | copy-start | bytes 442372
  4.5 13.3 %collective-permute-start.1 = (bf16[8,24,12,384]{3,1,2,0:T(8,128)(2,1)S(1)}, bf16[8,24,12,384]{3,1,2,0:T(8,128)(2,1)S(1)}, u32[]{:S(2)}, u32[]{:S(2)}) collective-permute-start(bf16[8,24,12,384]{3,1,2,0:T(8,128)(2,1)S(1)} %copy.10), channel_id=1, source_target_pairs={{1,0},{2,1},{3,2},{4,3},{5,4},{6,5},{7,6},{8,7},{9,8},{10,9},{11,1... | collective-permute-start | bytes 5308424 | tf_op jit(solution)/shard_map/ppermute | solution.py:47
  6.2 12.0 %collective-permute-start = (bf16[8,24,12,384]{3,1,2,0:T(8,128)(2,1)S(1)}, bf16[8,24,12,384]{3,1,2,0:T(8,128)(2,1)S(1)}, u32[]{:S(2)}, u32[]{:S(2)}) collective-permute-start(bf16[8,24,12,384]{3,1,2,0:T(8,128)(2,1)S(1)} %copy.9), channel_id=1, source_target_pairs={{0,1},{1,2},{2,3},{3,4},{4,5},{5,6},{6,7},{7,8},{8,9},{9,10},{10,1... | collective-permute-start | bytes 5308424 | tf_op jit(solution)/shard_map/ppermute | solution.py:46
  9.4 5.7 %collective-permute-start.2 = (bf16[8,12,384]{2,1,0:T(8,128)(2,1)S(1)}, bf16[8,12,384]{2,1,0:T(8,128)(2,1)S(1)}, u32[]{:S(2)}, u32[]{:S(2)}) collective-permute-start(bf16[8,12,384]{2,1,0:T(8,128)(2,1)S(1)} %get-tuple-element.16), channel_id=1, source_target_pairs={{0,1},{1,2},{2,3},{3,4},{4,5},{5,6},{6,7},{7,8},{8,9},{9,10},{10,1... | collective-permute-start | bytes 221192 | tf_op jit(solution)/shard_map/ppermute | solution.py:46
  13.8 3.2 %collective-permute-start.3 = (bf16[8,12,384]{2,1,0:T(8,128)(2,1)S(1)}, bf16[8,12,384]{2,1,0:T(8,128)(2,1)S(1)}, u32[]{:S(2)}, u32[]{:S(2)}) collective-permute-start(bf16[8,12,384]{2,1,0:T(8,128)(2,1)S(1)} %get-tuple-element.17), channel_id=1, source_target_pairs={{1,0},{2,1},{3,2},{4,3},{5,4},{6,5},{7,6},{8,7},{9,8},{10,9},{11,1... | collective-permute-start | bytes 221192 | tf_op jit(solution)/shard_map/ppermute | solution.py:47
  17.8 2.0 copy-start
  206.1 14.6 %collective-permute-start.4 = (bf16[24,9216]{1,0:T(8,128)(2,1)}, bf16[24,9216]{1,0:T(8,128)(2,1)S(1)}, u32[]{:S(2)}, u32[]{:S(2)}) collective-permute-start(bf16[24,9216]{1,0:T(8,128)(2,1)} %get-tuple-element.13), channel_id=1, source_target_pairs={{16,0},{17,1},{18,2},{19,3},{20,4},{21,5},{22,6},{23,7},{24,8},{25... | collective-permute-start | bytes 1327112 | tf_op jit(solution)/shard_map/ppermute | solution.py:364
  220.7 0.8 copy-start.2
